TPU v7x, 32 devices: a whole 2x2x4 slice. The times are simulated.
32 devices in a mesh: groups: 2 (over y), seq: 4 (over z), head: 2 (over x), sub: 2 (over core).
Axes of the slice: x: 2, y: 2, z: 4, core: 2. Of those that a mesh axis runs over, the one named last changes fastest.
Arguments:
- x_raw: bfloat16 [16, 128, 8192], P(('groups', 'seq', 'sub'), 'head'), parts along dimension 0, may hold values from -6 to 6
- bc_raw: bfloat16 [16, 128, 2048], P(('groups', 'seq', 'sub'), 'head'), parts along dimension 0, may hold values from -6 to 6
- dt_raw: bfloat16 [16, 128, 128], P(('groups', 'seq', 'sub'), 'head'), parts along dimension 0, may hold values from -3 to 40
- conv_x_weight: float32 [4, 8192], P(None, 'head'), may hold values from -3 to 3
- conv_x_bias: float32 [8192], P('head'), may hold values from -2.5 to 2.5
- conv_bc_weight: float32 [4, 2048], P(None, 'head'), may hold values from -3 to 3
- conv_bc_bias: float32 [2048], P('head'), may hold values from -2.5 to 2.5
- stride_offset_per_head: float32 [128], P('head'), may hold values from -12 to 0
- a_log: float32 [128], P('head'), may hold values from -8 to 3
- skip_d: float32 [128], P('head'), may hold values from 0.5 to 1.5
- norm_gain: float32 [8192], P('head'), may hold values from 0.1 to 1.9
Outputs:
- mixed: bfloat16 [16, 128, 8192], P(('groups', 'seq', 'sub'), None, 'head'), parts along dimension 0
There are 2 independent parts, one for each index of `groups`. A program takes and returns all parts, laid end to end along the dimension named above; an argument that names none is the same for every part. Nothing has to cross between parts.
All inputs are finite; a program needn't handle non-finite values.
Results may differ from a plain program's by a relative error of at most 0.0061.
Values may be sent and summed in bfloat16 or wider, within the bound.
No kernel may reach another device: no remote copies, remote signals or barrier semaphores. Data moves between devices by JAX's collectives and lax.ppermute only.
A program may use at most 128 MiB of HBM per device.

v0:
```python
import jax
import jax.numpy as jnp
from jax import lax
from jax.sharding import PartitionSpec as P

STATE = 128
SPAN = 128
NORM_EPSILON = 1e-05


def shifted(value, axis, steps):
    count = lax.axis_size(axis)
    leading, last = (max(0, -steps), min(count, count - steps))
    return lax.ppermute(value, axis, [(source, source + steps) for source in range(leading, last)])


def from_partner(shard, axis, distance):
    return lax.ppermute(shard, axis, [(i, i ^ 1 << distance) for i in range(lax.axis_size(axis))])


def prefix_2(shard, axis, combine, identity):
    length, position = (lax.axis_size(axis), lax.axis_index(axis))
    everything = jax.tree.map(lambda part: lax.all_gather(part, axis), shard)
    start = jax.tree.map(
        lambda part, zero: jnp.broadcast_to(jnp.asarray(zero, part.dtype), part.shape),
        shard,
        identity,
    )

    def hop(k, before):
        reached = k < position
        new = combine(before, jax.tree.map(lambda part: part[k], everything))
        return jax.tree.map(lambda a, b: jnp.where(reached, a, b), new, before)

    return lax.fori_loop(0, length, hop, start)


def conv_rows(raw_rows, rim_rows, weight, bias):
    conv_width = weight.shape[0]
    row_count = raw_rows.shape[0]
    joined = jnp.concatenate([rim_rows, raw_rows], axis=0).astype(jnp.float32)
    running = bias[None, :]
    for tap_index in range(conv_width):
        running = running + weight[tap_index][None, :] * joined[tap_index : tap_index + row_count]
    return jax.nn.silu(running).astype(jnp.bfloat16)


def chain_step(earlier, later_part):
    decay_early, state_early = earlier
    decay_later, state_later = later_part
    return (decay_early * decay_later, decay_later[..., None] * state_early + state_later)


def on_device(
    x_raw,
    bc_raw,
    dt_raw,
    conv_x_weight,
    conv_x_bias,
    conv_bc_weight,
    conv_bc_bias,
    stride_offset_per_head,
    a_log,
    skip_d,
    norm_gain,
):
    x_ex, bc_ex, dt_ex = (
        lax.all_to_all(x_raw, "head", split_axis=2, concat_axis=1, tiled=True),
        lax.all_to_all(bc_raw, "head", split_axis=2, concat_axis=1, tiled=True),
        lax.all_to_all(dt_raw, "head", split_axis=2, concat_axis=1, tiled=True),
    )
    x_rows = x_ex[0]
    bc_rows = bc_ex[0]
    dt_rows = dt_ex[0]
    conv_width = conv_x_weight.shape[0]
    x_rim, bc_rim = shifted(
        (x_rows[x_rows.shape[0] - conv_width + 1 :], bc_rows[bc_rows.shape[0] - conv_width + 1 :]),
        ("seq", "sub"),
        1,
    )
    x_conv = conv_rows(x_rows, x_rim, conv_x_weight, conv_x_bias)
    bc_conv = conv_rows(bc_rows, bc_rim, conv_bc_weight, conv_bc_bias)
    row_count = x_conv.shape[0]
    head_count = dt_rows.shape[1]
    groups = bc_conv.shape[1] // (2 * STATE)
    per_group = head_count // groups
    head_dim = x_conv.shape[1] // head_count
    group_width = per_group * head_dim
    span_len = SPAN
    blocks = row_count // span_len
    dt_step = jax.nn.softplus(dt_rows.astype(jnp.float32) + stride_offset_per_head[None, :])
    decay_rate = -jnp.exp(a_log)
    decay_logarithm_rows = (decay_rate[None, :] * dt_step).reshape(blocks, span_len, head_count)
    cum_decay = jnp.cumsum(decay_logarithm_rows, axis=1)
    step_blocks = dt_step.reshape(blocks, span_len, head_count)
    x_blocks = x_conv.reshape(blocks, span_len, groups, per_group, head_dim)
    x_wide = x_conv.reshape(blocks, span_len, groups, group_width)
    bc_blocks = bc_conv.reshape(blocks, span_len, groups, 2, STATE)
    b_in = bc_blocks[:, :, :, 0]
    c_out = bc_blocks[:, :, :, 1]

    def widen(per_head):
        return jnp.repeat(per_head, head_dim, axis=-1).reshape(
            per_head.shape[:-1] + (groups, group_width)
        )

    causal = lax.broadcasted_iota(jnp.int32, (span_len, span_len), 0) >= lax.broadcasted_iota(
        jnp.int32, (span_len, span_len), 1
    )
    inner_prod = jnp.einsum("btgn,bsgn->bgts", c_out, b_in, preferred_element_type=jnp.float32)
    cum_heads = jnp.transpose(cum_decay, (0, 2, 1)).reshape(blocks, groups, per_group, span_len)
    step_heads = jnp.transpose(step_blocks, (0, 2, 1)).reshape(blocks, groups, per_group, span_len)
    gap_pairs = cum_heads[..., :, None] - cum_heads[..., None, :]
    weight = jnp.exp(jnp.where(causal, gap_pairs, -1e30)) * step_heads[..., None, :]
    mixing = (inner_prod[:, :, None] * weight).astype(jnp.bfloat16)
    within_block_output = jnp.einsum(
        "bgjts,bsgjp->btgjp", mixing, x_blocks, preferred_element_type=jnp.float32
    )
    within_wide = within_block_output.reshape(blocks, span_len, groups, group_width)
    block_end = cum_decay[:, span_len - 1 :, :]
    to_end = jnp.exp(block_end - cum_decay) * step_blocks
    scaled = (widen(to_end) * x_wide).astype(jnp.bfloat16)
    states = jnp.einsum("bsgq,bsgn->bgqn", scaled, b_in, preferred_element_type=jnp.float32)
    decays = widen(jnp.exp(block_end[:, 0, :]))
    identity = (
        jnp.ones((groups, group_width), jnp.float32),
        jnp.zeros((groups, group_width, STATE), jnp.float32),
    )

    def local_step(running, block_item):
        return (chain_step(running, block_item), running)

    own_part, prefix = lax.scan(local_step, identity, (decays, states))
    partner = from_partner((own_part[0], own_part[1]), "sub", 0)
    is_lower = lax.axis_index("sub") == 0
    first_part = jax.tree.map(
        lambda mine, other: jnp.where(is_lower, mine, other), own_part, partner
    )
    second_part = jax.tree.map(
        lambda mine, other: jnp.where(is_lower, other, mine), own_part, partner
    )
    pair_total = chain_step(first_part, second_part)
    before_pair = prefix_2(pair_total, "seq", chain_step, identity)
    inside_pair = jax.tree.map(
        lambda empty, other: jnp.where(is_lower, empty, other), identity, partner
    )
    entry_part = chain_step(before_pair, inside_pair)
    device_entry = entry_part[1]
    carried = prefix[0][..., None] * device_entry[None] + prefix[1]
    carried_bf = carried.astype(jnp.bfloat16)
    y_state = jnp.einsum("btgn,bgqn->btgq", c_out, carried_bf, preferred_element_type=jnp.float32)
    y_state = y_state * widen(jnp.exp(cum_decay))
    skip_wide = jnp.repeat(skip_d, head_dim).reshape(groups, group_width)
    complete_output = within_wide + y_state + skip_wide * x_wide
    squares_mean = jnp.mean(complete_output * complete_output, axis=3)
    normed = (
        complete_output
        * lax.rsqrt(squares_mean + NORM_EPSILON)[..., None]
        * norm_gain.reshape(groups, group_width)
    )
    return normed.reshape(row_count, head_count * head_dim).astype(jnp.bfloat16)[None]


def solution(mesh):
    placed = (
        P(("groups", "seq", "sub"), "head", None),
        P(("groups", "seq", "sub"), "head", None),
        P(("groups", "seq", "sub"), "head", None),
        P(None, "head"),
        P("head"),
        P(None, "head"),
        P("head"),
        P("head"),
        P("head"),
        P("head"),
        P("head"),
    )
    return jax.shard_map(
        on_device,
        mesh=mesh,
        in_specs=placed,
        out_specs=P(("groups", "seq", "sub"), None, "head"),
        check_vma=False,
    )
```

profile of v0, /device:TPU:0, one launch (start us, length us, event | category | flops | bytes accessed | tf_op | source)
XLA Modules:
  0.0 315.5 jit_solution(2477985931013234938)
XLA Ops:
  9.6 4.2 %all-to-all-start.2 = ((bf16[2,2,2048]{2,1,0:T(2,128)(2,1)}), bf16[2,2,2048]{2,1,0:T(2,128)(2,1)S(1)}, u32[]{:S(2)}, u32[]{:S(2)}) async-start(bf16[2,2,2048]{2,1,0:T(2,128)(2,1)} %reshape.322), calls=%async_computation.2 | async-start | bytes 32768 | tf_op jit(solution)/shard_map/all_to_all | solution.py:70
  13.8 1.7 fusion.27
  17.0 9.2 %copy.48 = bf16[1,64,8192]{1,0,2:T(2,128)(2,1)} copy(bf16[1,64,8192]{2,1,0:T(8,128)(2,1)} %param.13) | data formatting | bytes 2097152 | tf_op args[0]
  26.2 45.3 %reduce.5 = bf16[8192,64]{1,0:T(8,128)(2,1)S(1)} reduce(bf16[8192,1,64]{2,1,0:T(2,128)(2,1)} %bitcast.99, bf16[]{:T(256)} %broadcast.182), dimensions={1}, to_apply=%bitcast.80.reduce_sub_computation | reduce | bytes 2097154
  71.5 2.4 reshape.320
  74.6 11.8 %reduce.7 = bf16[2048,64]{1,0:T(8,128)(2,1)S(1)} reduce(bf16[2048,1,64]{2,1,0:T(2,128)(2,1)S(1)} %bitcast.106, bf16[]{:T(256)} %broadcast.182), dimensions={1}, to_apply=%bitcast.84.reduce_sub_computation | reduce | bytes 524290
  87.5 3.4 %all-to-all-start.1 = ((bf16[2,2,32768]{2,1,0:T(2,128)(2,1)}), bf16[2,2,32768]{2,1,0:T(2,128)(2,1)S(1)}, u32[]{:S(2)}, u32[]{:S(2)}) async-start(bf16[2,2,32768]{2,1,0:T(2,128)(2,1)} %reshape.324), calls=%async_computation.1 | async-start | bytes 524288 | tf_op jit(solution)/shard_map/all_to_all | solution.py:69
  92.6 4.0 %all-to-all-done.1 = bf16[2,2,32768]{2,1,0:T(2,128)(2,1)S(1)} async-done(((bf16[2,2,32768]{2,1,0:T(2,128)(2,1)}), bf16[2,2,32768]{2,1,0:T(2,128)(2,1)S(1)}, u32[]{:S(2)}, u32[]{:S(2)}) %all-to-all-start.1) | async-done | bytes 262176 | tf_op jit(solution)/shard_map/all_to_all | solution.py:69
  96.6 3.6 %all-to-all-start = ((bf16[2,2,131072]{2,1,0:T(2,128)(2,1)}), bf16[2,2,131072]{2,1,0:T(2,128)(2,1)S(1)}, u32[]{:S(2)}, u32[]{:S(2)}) async-start(bf16[2,2,131072]{2,1,0:T(2,128)(2,1)} %reshape.320), calls=%async_computation | async-start | bytes 2097152 | tf_op jit(solution)/shard_map/all_to_all | solution.py:68
  102.3 1.3 collective-permute-start.1
  104.5 8.9 %all-to-all-done = bf16[2,2,131072]{2,1,0:T(2,128)(2,1)S(1)} async-done(((bf16[2,2,131072]{2,1,0:T(2,128)(2,1)}), bf16[2,2,131072]{2,1,0:T(2,128)(2,1)S(1)}, u32[]{:S(2)}, u32[]{:S(2)}) %all-to-all-start) | async-done | bytes 1048608 | tf_op jit(solution)/shard_map/all_to_all | solution.py:68
  113.4 2.7 reshape.321
  116.2 8.2 %copy.49 = bf16[1,64,8192]{2,1,0:T(8,128)(2,1)S(1)} copy(bf16[1,64,8192]{1,0,2:T(2,128)(2,1)} %bitcast.98) | data formatting | bytes 2097152 | tf_op jit(solution)/shard_map/all_to_all | solution.py:68
  125.8 1.3 collective-permute-start
  128.3 1.3 multiply_convert_fusion.3
  132.6 2.6 collective-permute-start.3
  135.1 3.8 %collective-permute-done.3 = f32[4,1024,128]{2,1,0:T(8,128)S(1)} collective-permute-done((f32[4,1024,128]{2,1,0:T(8,128)S(1)}, f32[4,1024,128]{2,1,0:T(8,128)S(1)}, u32[]{:S(2)}, u32[]{:S(2)}) %collective-permute-start.3) | collective-permute-done | bytes 2097184 | tf_op jit(solution)/shard_map/ppermute | solution.py:18
  138.9 1.3 copy-done.2
  140.3 1.7 select_add_fusion
  144.2 1.3 mul.290
  147.5 15.4 %all-gather.2 = f32[4,4,1024]{2,1,0:T(4,128)S(1)} all-gather(f32[1,4,1024]{2,1,0:T(4,128)} %get-tuple-element.160), channel_id=2, replica_groups=mesh['groups'=2,'seq'=4,'head'=2,'sub'=2] {'seq'}, dimensions={0}, use_global_device_ids=true | all-gather | bytes 81920 | tf_op jit(solution)/shard_map/all_gather | solution.py:23
  163.8 1.3 copy.51
  165.1 3.9 %fusion.1 = f32[4,16,64,128]{3,2,1,0:T(8,128)} fusion(bf16[128,4,16,64]{0,3,2,1:T(8,128)(2,1)} %bitcast.114, f32[4,16,128]{2,1,0:T(8,128)S(1)} %bitcast.124, f32[4,16,128]{2,1,0:T(8,128)S(1)} %bitcast.125, f32[4,128,128]{2,1,0:T(8,128)} %fusion.22, pred[128,128]{1,0:T(8,128)(4,1)} %iota_compare_fusion), kind=kOutput, calls=%fused_computation.4 | convolution fusion | flops 139460608 | bytes 3489792 | tf_op jit(solution)/shard_map/bgjts,bsgjp->btgjp/dot_general | solution.py:116
  169.0 124.5 %all-gather.5.cloned.1.call-done = f32[16,1024,128]{2,1,0:T(8,128)} async-done(((f32[4,1024,128]{2,1,0:T(8,128)}), f32[16,1024,128]{2,1,0:T(8,128)}) %all-gather.5.cloned.1.call-update) | async-done | bytes 8388624 | tf_op jit(solution)/shard_map/all_gather | solution.py:23
  293.5 8.8 %while.9 = (s32[]{:T(128)}, f32[4,1024,128]{2,1,0:T(8,128)S(1)}, s32[]{:T(128)}, f32[4,4,1024]{2,1,0:T(4,128)S(1)}, f32[4,4,1024,128]{3,2,1,0:T(8,128)}, /*index=5*/s32[]{:T(128)}, s32[]{:T(128)}) while((s32[]{:T(128)}, f32[4,1024,128]{2,1,0:T(8,128)S(1)}, s32[]{:T(128)}, f32[4,4,1024]{2,1,0:T(4,128)S(1)}, ...), condition=%wide.region_2.3_spmd.clone, body=%wide.region_1.2_spmd.clone.sunk | while | flops 2097156 | bytes 6340713 | solution.py:35
  293.5 2.2 fusion.32
  295.7 2.2 fusion.32
  297.9 2.2 fusion.32
  300.1 2.2 fusion.32
  302.5 1.4 copy-done.1
  303.9 2.6 multiply_reduce_fusion
  307.3 1.3 copy.67
  (94 shorter events, 22.4 us)
Async XLA Ops:
  9.6 78.0 %all-to-all-start.2 = ((bf16[2,2,2048]{2,1,0:T(2,128)(2,1)}), bf16[2,2,2048]{2,1,0:T(2,128)(2,1)S(1)}, u32[]{:S(2)}, u32[]{:S(2)}) async-start(bf16[2,2,2048]{2,1,0:T(2,128)(2,1)} %reshape.322), calls=%async_computation.2 | async-start | bytes 32768 | tf_op jit(solution)/shard_map/all_to_all | solution.py:70
  71.5 2.5 copy-start.3
  73.9 17.4 %copy-start.16 = (f32[64]{0:T(128)S(1)}, f32[64]{0:T(128)}, u32[]{:S(2)}) copy-start(f32[64]{0:T(128)} %param.20) | copy-start | bytes 772
  87.5 9.1 %all-to-all-start.1 = ((bf16[2,2,32768]{2,1,0:T(2,128)(2,1)}), bf16[2,2,32768]{2,1,0:T(2,128)(2,1)S(1)}, u32[]{:S(2)}, u32[]{:S(2)}) async-start(bf16[2,2,32768]{2,1,0:T(2,128)(2,1)} %reshape.324), calls=%async_computation.1 | async-start | bytes 524288 | tf_op jit(solution)/shard_map/all_to_all | solution.py:69
  92.6 11.1 %collective-permute-start.2 = (f32[4,1024]{1,0:T(4,128)S(1)}, f32[4,1024]{1,0:T(4,128)S(1)}, u32[]{:S(2)}, u32[]{:S(2)}) collective-permute-start(f32[4,1024]{1,0:T(4,128)S(1)} %broadcast_in_dim.63), channel_id=1, source_target_pairs={{0,1},{1,0},{2,3},{3,2},{4,5},{5,4},{6,7},{7,6},{8,9},{9,8},{10,11... | collective-permute-start | bytes 49160 | tf_op jit(solution)/shard_map/ppermute | solution.py:18
  96.6 16.8 %all-to-all-start = ((bf16[2,2,131072]{2,1,0:T(2,128)(2,1)}), bf16[2,2,131072]{2,1,0:T(2,128)(2,1)S(1)}, u32[]{:S(2)}, u32[]{:S(2)}) async-start(bf16[2,2,131072]{2,1,0:T(2,128)(2,1)} %reshape.320), calls=%async_computation | async-start | bytes 2097152 | tf_op jit(solution)/shard_map/all_to_all | solution.py:68
  100.2 193.3 %all-gather.5.cloned.1.call-start = ((), (), s32[]{:S(2)}) async-start(), calls=%async_computation.3 | async-start | bytes 10485760 | tf_op jit(solution)/shard_map/all_gather | solution.py:23
  102.3 2.1 collective-permute-start.1
  124.4 2.7 copy-start.15
  125.8 2.1 collective-permute-start
  127.5 0.8 copy-start.8
  127.5 0.8 copy-start.9
  127.5 0.8 copy-start.10
  127.5 0.8 copy-start.11
  127.5 0.8 copy-start.14
  130.2 1.4 copy-start
  131.1 0.7 copy-start.7
  132.6 6.4 %collective-permute-start.3 = (f32[4,1024,128]{2,1,0:T(8,128)S(1)}, f32[4,1024,128]{2,1,0:T(8,128)S(1)}, u32[]{:S(2)}, u32[]{:S(2)}) collective-permute-start(f32[4,1024,128]{2,1,0:T(8,128)S(1)} %convolution_add_fusion), channel_id=1, source_target_pairs={{0,1},{1,0},{2,3},{3,2},{4,5},{5,4},{6,7},{7,6},{8,9},{9,8},{10,11... | collective-permute-start | bytes 6291464 | tf_op jit(solution)/shard_map/ppermute | solution.py:18
  138.9 1.3 copy-start.2
  141.9 0.7 copy-start.17
  147.5 17.6 %copy-start.12 = (f32[1,128,64]{1,2,0:T(8,128)S(1)}, f32[1,128,64]{1,2,0:T(8,128)}, u32[]{:S(2)}) copy-start(f32[1,128,64]{1,2,0:T(8,128)} %get-tuple-element.150) | copy-start | bytes 98308
  147.5 17.6 %copy-start.13 = (f32[1,64,128]{2,1,0:T(8,128)S(1)}, f32[1,64,128]{2,1,0:T(8,128)}, u32[]{:S(2)}) copy-start(f32[1,64,128]{2,1,0:T(8,128)} %copy.62) | copy-start | bytes 98308
  293.5 8.8 %copy-start.4 = (f32[128,64]{0,1:T(8,128)S(1)}, f32[128,64]{0,1:T(8,128)}, u32[]{:S(2)}) copy-start(f32[128,64]{0,1:T(8,128)} %copy.65) | copy-start | bytes 98308
  302.3 1.6 copy-start.1
  302.3 1.6 copy-start.6
  303.9 2.7 copy-start.5
Sparse Core Ops, SparseCore 0:
  142.1 151.4 all-gather.4
where the time goes:
time: 317 us; the launch traced here: 315 us
  waiting for transfers between devices  142 us (45%)
  other arithmetic  74.1 us (23%)
  local copies, waits for them, and re-layouts  45.6 us (14%)
  starting transfers between devices  16.5 us (5%)
  blocking collectives  15.4 us (5%)
  between operations  13.9 us (4%)
  matrix products  8.22 us (3%)
    all_gather x1, waiting for transfers between devices, prefix_2(): everything = jax.tree.map(lambda part: lax.all_gather(part, axis), shard)  125 us
    unnamed x4, other arithmetic  57.9 us
    unnamed x46, local copies, waits for them, and re-layouts  22.8 us
    all_gather x1, blocking collectives, prefix_2(): everything = jax.tree.map(lambda part: lax.all_gather(part, axis), shard)  15.4 us
    all_to_all x3, local copies, waits for them, and re-layouts, on_device(): lax.all_to_all(x_raw, 'head', split_axis=2, concat_axis=1, tiled=True)  9.54 us
    all_to_all x1, waiting for transfers between devices, on_device(): lax.all_to_all(x_raw, 'head', split_axis=2, concat_axis=1, tiled=True)  8.91 us
    select_n x4, other arithmetic, hop(): return jax.tree.map(lambda a, b: jnp.where(reached, a, b), new, before)  8.64 us
  transfers between devices with their start and end apart: 8, of which 6 were waited for; matrix products, arithmetic and copies ran while one was open for 28% of the time, Pallas kernels for 0%

commit v1 on v0

--- a/solution.py
+++ b/solution.py
@@ -65,7 +65,12 @@
     norm_gain,
 ):
     x_ex, bc_ex, dt_ex = (
-        lax.all_to_all(x_raw, "head", split_axis=2, concat_axis=1, tiled=True),
+        jnp.concatenate(
+            lax.all_to_all(
+                jnp.stack(jnp.split(x_raw, lax.axis_size("head"), axis=2)), "head", 0, 0
+            ),
+            axis=1,
+        ),
         lax.all_to_all(bc_raw, "head", split_axis=2, concat_axis=1, tiled=True),
         lax.all_to_all(dt_raw, "head", split_axis=2, concat_axis=1, tiled=True),
     )

time: 317 us -> 247 us (0.78)
  other arithmetic: 74.1 us -> 29.1 us
  local copies, waits for them, and re-layouts: 45.6 us -> 21.4 us
    unnamed x4 -> x3, other arithmetic: 57.9 us -> 12.5 us
    unnamed x46 -> x49, local copies, waits for them, and re-layouts: 22.8 us -> 8.67 us
    all_to_all x3 -> x0, local copies, waits for them, and re-layouts: 9.54 us -> none  [on_device(): lax.all_to_all(x_raw, 'head', split_axis=2, concat_axis=1, tiled=True)]
  transfers between devices with their start and end apart: 8 -> 8, of which waited for: 6 -> 6; matrix products, arithmetic and copies ran while one was open for 28% -> 13% of each run, Pallas kernels for 0% -> 0%
where the time goes in v1:
time: 247 us; the launch traced here: 246 us
  waiting for transfers between devices  141 us (57%)
  other arithmetic  29.1 us (12%)
  local copies, waits for them, and re-layouts  21.4 us (9%)
  starting transfers between devices  16.5 us (7%)
  blocking collectives  15.4 us (6%)
  between operations  13.8 us (6%)
  matrix products  8.2 us (3%)
    all_gather x1, waiting for transfers between devices, prefix_2(): everything = jax.tree.map(lambda part: lax.all_gather(part, axis), shard)  124 us
    all_gather x1, blocking collectives, prefix_2(): everything = jax.tree.map(lambda part: lax.all_gather(part, axis), shard)  15.4 us
    unnamed x3, other arithmetic  12.5 us
    all_to_all x1, waiting for transfers between devices, on_device(): lax.all_to_all(jnp.stack(jnp.split(x_raw, lax.axis_size('head'), axis=2))...  8.92 us
    unnamed x49, local copies, waits for them, and re-layouts  8.67 us
    select_n x4, other arithmetic, hop(): return jax.tree.map(lambda a, b: jnp.where(reached, a, b), new, before)  8.64 us
  transfers between devices with their start and end apart: 8, of which 6 were waited for; matrix products, arithmetic and copies ran while one was open for 13% of the time, Pallas kernels for 0%

profile of v1, /device:TPU:0, one launch (start us, length us, event | category | flops | bytes accessed | tf_op | source)
XLA Modules:
  0.0 246.0 jit_solution(8992217306841146224)
XLA Ops:
  8.0 0.9 reduce.5
  9.6 4.2 %all-to-all-start.2 = ((bf16[2,2,2048]{2,1,0:T(2,128)(2,1)}), bf16[2,2,2048]{2,1,0:T(2,128)(2,1)S(1)}, u32[]{:S(2)}, u32[]{:S(2)}) async-start(bf16[2,2,2048]{2,1,0:T(2,128)(2,1)} %reshape.319), calls=%async_computation.2 | async-start | bytes 32768 | tf_op jit(solution)/shard_map/all_to_all | solution.py:75
  13.8 1.3 slice_bitcast_fusion.1
  15.8 1.1 pad_maximum_fusion
  17.6 11.6 %reduce.6 = bf16[2048,64]{1,0:T(8,128)(2,1)S(1)} reduce(bf16[2048,1,64]{2,1,0:T(2,128)(2,1)S(1)} %bitcast.105, bf16[]{:T(256)} %broadcast.182), dimensions={1}, to_apply=%bitcast.85.reduce_sub_computation | reduce | bytes 524290
  29.2 1.1 reshape.321
  30.3 3.4 %all-to-all-start.1 = ((bf16[2,2,32768]{2,1,0:T(2,128)(2,1)}), bf16[2,2,32768]{2,1,0:T(2,128)(2,1)S(1)}, u32[]{:S(2)}, u32[]{:S(2)}) async-start(bf16[2,2,32768]{2,1,0:T(2,128)(2,1)} %reshape.321), calls=%async_computation.1 | async-start | bytes 524288 | tf_op jit(solution)/shard_map/all_to_all | solution.py:74
  35.4 4.0 %all-to-all-done.1 = bf16[2,2,32768]{2,1,0:T(2,128)(2,1)S(1)} async-done(((bf16[2,2,32768]{2,1,0:T(2,128)(2,1)}), bf16[2,2,32768]{2,1,0:T(2,128)(2,1)S(1)}, u32[]{:S(2)}, u32[]{:S(2)}) %all-to-all-start.1) | async-done | bytes 262176 | tf_op jit(solution)/shard_map/all_to_all | solution.py:74
  39.5 3.6 %all-to-all-start = ((bf16[2,1,64,4096]{3,2,1,0:T(8,128)(2,1)}), bf16[2,1,64,4096]{3,2,1,0:T(8,128)(2,1)S(1)}, u32[]{:S(2)}, u32[]{:S(2)}) async-start(bf16[2,1,64,4096]{3,2,1,0:T(8,128)(2,1)} %pad_maximum_fusion), calls=%async_computation | async-start | bytes 2097152 | tf_op jit(solution)/shard_map/all_to_all | solution.py:69
  45.2 1.3 collective-permute-start.1
  47.4 8.9 %all-to-all-done = bf16[2,1,64,4096]{3,2,1,0:T(8,128)(2,1)S(1)} async-done(((bf16[2,1,64,4096]{3,2,1,0:T(8,128)(2,1)}), bf16[2,1,64,4096]{3,2,1,0:T(8,128)(2,1)S(1)}, u32[]{:S(2)}, u32[]{:S(2)}) %all-to-all-start) | async-done | bytes 1048608 | tf_op jit(solution)/shard_map/all_to_all | solution.py:69
  56.3 1.5 collective-permute-start
  59.0 1.3 multiply_convert_fusion.3
  60.8 0.9 broadcast_in_dim.66
  63.2 2.4 collective-permute-start.3
  65.6 3.8 %collective-permute-done.3 = f32[4,1024,128]{2,1,0:T(8,128)S(1)} collective-permute-done((f32[4,1024,128]{2,1,0:T(8,128)S(1)}, f32[4,1024,128]{2,1,0:T(8,128)S(1)}, u32[]{:S(2)}, u32[]{:S(2)}) %collective-permute-start.3) | collective-permute-done | bytes 2097184 | tf_op jit(solution)/shard_map/ppermute | solution.py:18
  69.4 1.3 copy-done.2
  70.8 1.7 select_add_fusion
  74.7 1.3 mul.290
  78.1 15.4 %all-gather.2 = f32[4,4,1024]{2,1,0:T(4,128)S(1)} all-gather(f32[1,4,1024]{2,1,0:T(4,128)} %get-tuple-element.162), channel_id=2, replica_groups=mesh['groups'=2,'seq'=4,'head'=2,'sub'=2] {'seq'}, dimensions={0}, use_global_device_ids=true | all-gather | bytes 81920 | tf_op jit(solution)/shard_map/all_gather | solution.py:23
  93.5 0.9 fusion.22
  94.4 1.3 copy.97
  95.7 3.9 %fusion.1 = f32[4,16,64,128]{3,2,1,0:T(8,128)} fusion(bf16[128,4,16,64]{0,3,2,1:T(8,128)(2,1)} %bitcast.112, f32[4,16,128]{2,1,0:T(8,128)S(1)} %bitcast.122, f32[4,16,128]{2,1,0:T(8,128)S(1)} %bitcast.123, f32[4,128,128]{2,1,0:T(8,128)} %fusion.22, pred[128,128]{1,0:T(8,128)(4,1)} %iota_compare_fusion), kind=kOutput, calls=%fused_computation.4 | convolution fusion | flops 139460608 | bytes 3489792 | tf_op jit(solution)/shard_map/bgjts,bsgjp->btgjp/dot_general | solution.py:121
  99.6 124.5 %all-gather.5.cloned.1.call-done = f32[16,1024,128]{2,1,0:T(8,128)} async-done(((f32[4,1024,128]{2,1,0:T(8,128)}), f32[16,1024,128]{2,1,0:T(8,128)}) %all-gather.5.cloned.1.call-update) | async-done | bytes 8388624 | tf_op jit(solution)/shard_map/all_gather | solution.py:23
  224.1 8.8 %while.9 = (s32[]{:T(128)}, f32[4,1024,128]{2,1,0:T(8,128)S(1)}, s32[]{:T(128)}, f32[4,4,1024]{2,1,0:T(4,128)S(1)}, f32[4,4,1024,128]{3,2,1,0:T(8,128)}, /*index=5*/s32[]{:T(128)}, s32[]{:T(128)}) while((s32[]{:T(128)}, f32[4,1024,128]{2,1,0:T(8,128)S(1)}, s32[]{:T(128)}, f32[4,4,1024]{2,1,0:T(4,128)S(1)}, ...), condition=%wide.region_2.3_spmd.clone, body=%wide.region_1.2_spmd.clone.sunk | while | flops 2097156 | bytes 6340713 | solution.py:35
  224.1 2.2 fusion.32
  226.3 2.2 fusion.32
  228.5 2.2 fusion.32
  230.7 2.2 fusion.32
  233.0 1.4 copy-done.1
  234.5 2.6 %multiply_reduce_fusion = (f32[128,4]{0,1:T(4,128)S(1)}, f32[1,128,4,1024]{1,3,2,0:T(8,128)S(1)}) fusion(f32[1,128,4,1024]{1,3,2,0:T(8,128)S(1)} %bitcast.98, f32[4,1024]{1,0:T(4,128)S(1)} %broadcast_in_dim.72, f32[1,128,4,1024]{1,3,2,0:T(8,128)S(1)} %bitcast.101, bf16[1,128,4,2,128]{1,4,3,2,0:T(8,128)(2,1)S(1)} %bitcast.109, ...), kind=kOutput, calls=%fused_computation.19 | convolution fusion | flops 139460096 | bytes 12748801 | tf_op jit(solution)/shard_map/btgn,bgqn->btgq/dot_general | solution.py:156
  237.9 1.3 copy.113
  (95 shorter events, 16.4 us)
Async XLA Ops:
  6.5 8.6 %copy-start.12 = (f32[4,4096]{1,0:T(4,128)S(1)}, f32[4,4096]{1,0:T(4,128)}, u32[]{:S(2)}) copy-start(f32[4,4096]{1,0:T(4,128)} %param.16) | copy-start | bytes 196612
  6.5 9.3 %copy-start.16 = (f32[4,1024]{1,0:T(4,128)S(1)}, f32[4,1024]{1,0:T(4,128)}, u32[]{:S(2)}) copy-start(f32[4,1024]{1,0:T(4,128)} %param.18) | copy-start | bytes 49156
  9.6 20.8 %all-to-all-start.2 = ((bf16[2,2,2048]{2,1,0:T(2,128)(2,1)}), bf16[2,2,2048]{2,1,0:T(2,128)(2,1)S(1)}, u32[]{:S(2)}, u32[]{:S(2)}) async-start(bf16[2,2,2048]{2,1,0:T(2,128)(2,1)} %reshape.319), calls=%async_computation.2 | async-start | bytes 32768 | tf_op jit(solution)/shard_map/all_to_all | solution.py:75
  13.8 3.1 %copy-start.20 = (f32[64]{0:T(128)S(1)}, f32[64]{0:T(128)}, u32[]{:S(2)}) copy-start(f32[64]{0:T(128)} %param.21) | copy-start | bytes 772
  13.8 3.1 %copy-start.3 = (bf16[1,64,2048]{2,1,0:T(8,128)(2,1)S(1)}, bf16[1,64,2048]{2,1,0:T(8,128)(2,1)}, u32[]{:S(2)}) copy-start(bf16[1,64,2048]{2,1,0:T(8,128)(2,1)} %param.14) | copy-start | bytes 786436
  16.9 17.3 %copy-start.18 = (f32[64]{0:T(128)S(1)}, f32[64]{0:T(128)}, u32[]{:S(2)}) copy-start(f32[64]{0:T(128)} %param.20) | copy-start | bytes 772
  30.3 9.1 %all-to-all-start.1 = ((bf16[2,2,32768]{2,1,0:T(2,128)(2,1)}), bf16[2,2,32768]{2,1,0:T(2,128)(2,1)S(1)}, u32[]{:S(2)}, u32[]{:S(2)}) async-start(bf16[2,2,32768]{2,1,0:T(2,128)(2,1)} %reshape.321), calls=%async_computation.1 | async-start | bytes 524288 | tf_op jit(solution)/shard_map/all_to_all | solution.py:74
  35.4 11.1 %collective-permute-start.2 = (f32[4,1024]{1,0:T(4,128)S(1)}, f32[4,1024]{1,0:T(4,128)S(1)}, u32[]{:S(2)}, u32[]{:S(2)}) collective-permute-start(f32[4,1024]{1,0:T(4,128)S(1)} %broadcast_in_dim.63), channel_id=1, source_target_pairs={{0,1},{1,0},{2,3},{3,2},{4,5},{5,4},{6,7},{7,6},{8,9},{9,8},{10,11... | collective-permute-start | bytes 49160 | tf_op jit(solution)/shard_map/ppermute | solution.py:18
  39.5 16.8 %all-to-all-start = ((bf16[2,1,64,4096]{3,2,1,0:T(8,128)(2,1)}), bf16[2,1,64,4096]{3,2,1,0:T(8,128)(2,1)S(1)}, u32[]{:S(2)}, u32[]{:S(2)}) async-start(bf16[2,1,64,4096]{3,2,1,0:T(8,128)(2,1)} %pad_maximum_fusion), calls=%async_computation | async-start | bytes 2097152 | tf_op jit(solution)/shard_map/all_to_all | solution.py:69
  43.1 181.0 %all-gather.5.cloned.1.call-start = ((), (), s32[]{:S(2)}) async-start(), calls=%async_computation.3 | async-start | bytes 10485760 | tf_op jit(solution)/shard_map/all_gather | solution.py:23
  43.9 13.9 %copy-start.17 = (f32[1024]{0:T(1024)S(1)}, f32[1024]{0:T(1024)}, u32[]{:S(2)}) copy-start(f32[1024]{0:T(1024)} %param.19) | copy-start | bytes 12292
  45.2 2.1 collective-permute-start.1
  56.3 2.1 collective-permute-start
  58.2 0.7 copy-start.8
  58.2 0.7 copy-start.9
  58.2 0.7 copy-start.10
  58.2 0.7 copy-start.11
  58.2 0.7 copy-start.15
  60.8 1.4 copy-start
  61.8 0.7 copy-start.7
  63.2 6.2 %collective-permute-start.3 = (f32[4,1024,128]{2,1,0:T(8,128)S(1)}, f32[4,1024,128]{2,1,0:T(8,128)S(1)}, u32[]{:S(2)}, u32[]{:S(2)}) collective-permute-start(f32[4,1024,128]{2,1,0:T(8,128)S(1)} %convolution_add_fusion), channel_id=1, source_target_pairs={{0,1},{1,0},{2,3},{3,2},{4,5},{5,4},{6,7},{7,6},{8,9},{9,8},{10,11... | collective-permute-start | bytes 6291464 | tf_op jit(solution)/shard_map/ppermute | solution.py:18
  69.4 1.3 copy-start.2
  72.5 0.7 copy-start.19
  78.1 17.6 %copy-start.13 = (f32[1,128,64]{1,2,0:T(8,128)S(1)}, f32[1,128,64]{1,2,0:T(8,128)}, u32[]{:S(2)}) copy-start(f32[1,128,64]{1,2,0:T(8,128)} %get-tuple-element.150) | copy-start | bytes 98308
  78.1 17.6 %copy-start.14 = (f32[1,64,128]{2,1,0:T(8,128)S(1)}, f32[1,64,128]{2,1,0:T(8,128)}, u32[]{:S(2)}) copy-start(f32[1,64,128]{2,1,0:T(8,128)} %copy.108) | copy-start | bytes 98308
  224.1 8.8 %copy-start.4 = (f32[128,64]{0,1:T(8,128)S(1)}, f32[128,64]{0,1:T(8,128)}, u32[]{:S(2)}) copy-start(f32[128,64]{0,1:T(8,128)} %copy.111) | copy-start | bytes 98308
  232.9 1.6 copy-start.1
  232.9 1.6 copy-start.6
  234.5 2.7 %copy-start.5 = (f32[4,1024]{1,0:T(4,128)S(1)}, f32[4,1024]{1,0:T(4,128)}, u32[]{:S(2)}) copy-start(f32[4,1024]{1,0:T(4,128)} %mul.290) | copy-start | bytes 49156
Sparse Core Ops, SparseCore 0:
  72.6 151.4 all-gather.4
